TPU v7x, 32 devices: a whole 2x2x4 slice. The times are simulated.
32 devices in a mesh: side: 2 (over core), group: 8 (over z, y), head: 2 (over x).
Axes of the slice: x: 2, y: 2, z: 4, core: 2. Of those that a mesh axis runs over, the one named last changes fastest.
Arguments:
- pool_rows: bfloat16 [2, 768, 4096], P('side', ('group', 'head')), may hold values from -24 to 24
- pool_weight: bfloat16 [2, 4096, 8192], P('side', 'group', 'head'), as said below
- lengths: int32 [8, 3], replicated, may hold values from 1 to 48, 96 in all within a row
- owner: int32 [8, 3], replicated, may hold values from 0 to 7, as said below
Outputs:
- pool_out: bfloat16 [2, 768, 4096], P('side', 'group', 'head')
Inputs may be any that keep to these rules, and one draw needn't show every extreme that they name: owner[p, j] is p with the binary digits of m_j flipped, where m_j = owner[0, j] is the same for every p; the m_j differ between slots, and every binary digit below 8 is set in some m_j. So the 3 requests of a prefill group go to different decode groups, and every decode group receives exactly one request for each slot j. `lengths`: each row sums to 96. `pool_weight`: independent normal entries of deviation 1 / sqrt(4096).
All inputs are finite; a program needn't handle non-finite values.
Results may differ from a plain program's by a relative error of at most 0.0061.
Values may be sent and summed in bfloat16 or wider, within the bound.
A program may use at most 128 MiB of HBM per device.

v0:
```python
import jax
import jax.numpy as jnp
from jax import lax
from jax.sharding import PartitionSpec as P

HEAD_DIM = 256


def shifted(value, axis, by):
    count = lax.axis_size(axis)
    pairs = [(i, i + by) for i in range(count) if 0 <= i + by < count]
    return lax.ppermute(value, axis, pairs)


def on_device(pool_rows, pool_weight, lengths, owner):
    side_index = lax.axis_index("side")
    group_index = lax.axis_index("group")
    requests = lengths.shape[1]
    gathered = lax.all_gather(pool_rows[0], "head", axis=0, tiled=True)
    weight = lax.all_gather(pool_weight[0], "group", axis=0, tiled=True)
    mem_g = gathered.shape[0]
    wide = weight.shape[1] // 2
    heads_dev = wide // HEAD_DIM
    q_req = mem_g // requests
    scale = 1.0 / HEAD_DIM**0.5
    cached = jnp.dot(gathered, weight, preferred_element_type=jnp.float32).astype(jnp.bfloat16)
    queries = cached[:, :wide]
    starts = jnp.cumsum(lengths, axis=1) - lengths
    groups = jnp.arange(lengths.shape[0], dtype=jnp.int32)
    sources, begins, counts = ([], [], [])
    for slot in range(requests):
        hit = owner[:, slot] == group_index
        sources.append(jnp.sum(jnp.where(hit, groups, 0)))
        begins.append(jnp.sum(jnp.where(hit, starts[:, slot], 0)))
        counts.append(jnp.sum(jnp.where(hit, lengths[:, slot], 0)))
    moved = shifted(cached, "side", 1)
    row_slot = jnp.arange(mem_g, dtype=jnp.int32) // q_req
    lower = jnp.zeros((mem_g,), jnp.int32)
    upper = jnp.zeros((mem_g,), jnp.int32)
    for slot in range(requests):
        here = row_slot == slot
        first_row = sources[slot] * mem_g + begins[slot]
        lower = jnp.where(here, first_row, lower)
        upper = jnp.where(here, first_row + counts[slot], upper)
    query_heads = queries.reshape(mem_g, heads_dev, HEAD_DIM)
    piece = lax.all_gather(moved, "group", axis=0, tiled=True)
    running = jnp.full((heads_dev, mem_g), -1e30, jnp.float32)
    count_rows = piece.shape[0]
    key_index = jnp.arange(count_rows, dtype=jnp.int32)
    key_rows = piece[:, :wide].reshape(count_rows, heads_dev, HEAD_DIM)
    value_rows = piece[:, wide:].reshape(count_rows, heads_dev, HEAD_DIM)
    allowed = (key_index[None, :] >= lower[:, None]) & (key_index[None, :] < upper[:, None])
    scores = (
        jnp.einsum("qeh,keh->eqk", query_heads, key_rows, preferred_element_type=jnp.float32)
        * scale
    )
    scores = jnp.where(allowed[None], scores, -1e30)
    newest = jnp.maximum(running, jnp.max(scores, axis=-1))
    expo = jnp.where(allowed[None], jnp.exp(scores - newest[:, :, None]), 0.0)
    total = jnp.sum(expo, axis=-1)
    update = jnp.einsum(
        "eqk,keh->eqh", expo.astype(jnp.bfloat16), value_rows, preferred_element_type=jnp.float32
    )
    accum = update
    running, total, accum = (newest, total, accum)
    mixed = accum / total[:, :, None]
    attended = jnp.transpose(mixed, (1, 0, 2)).reshape(mem_g, wide).astype(jnp.bfloat16)
    partial_out = lax.dot_general(
        attended, weight[:, wide:], (((1,), (1,)), ((), ())), preferred_element_type=jnp.float32
    )
    decoded = lax.psum_scatter(partial_out, "head", scatter_dimension=1, tiled=True).astype(
        jnp.bfloat16
    )
    result = jnp.where(side_index == 0, cached[:, :wide], decoded)
    return result[None]


def solution(mesh):
    placed = (P("side", ("group", "head"), None), P("side", "group", "head"), P(), P())
    return jax.shard_map(
        on_device, mesh=mesh, in_specs=placed, out_specs=P("side", "group", "head"), check_vma=False
    )
```

profile of v0, /device:TPU:0, one launch (start us, length us, event | category | flops | bytes accessed | tf_op | source)
XLA Modules:
  0.0 815.8 jit_solution(10971161938531449910)
XLA Ops:
  6.5 0.0 copy-start.1
  6.5 0.0 all-gather.7.cloned.1.call-start
  6.5 0.7 all-gather.7.cloned.1.call-update
  7.3 0.0 all-gather.5.cloned.1.call-start
  7.3 0.2 copy-done.1
  7.5 12.7 %all-gather = bf16[1,96,4096]{2,1,0:T(8,128)(2,1)S(1)} all-gather(bf16[1,48,4096]{2,1,0:T(8,128)(2,1)S(1)} %copy-done.1), channel_id=2, replica_groups=mesh['side'=2,'group'=8,'head'=2] {'head'}, dimensions={1}, use_global_device_ids=true | all-gather | bytes 1179648 | tf_op jit(solution)/shard_map/all_gather | solution.py:19
  20.3 0.0 copy-start.2
  20.3 0.0 copy-start.3
  20.3 629.0 %all-gather.7.cloned.1.call-done = bf16[1,4096,4096]{2,1,0:T(8,128)(2,1)} async-done(((bf16[1,512,4096]{2,1,0:T(8,128)(2,1)}), bf16[1,4096,4096]{2,1,0:T(8,128)(2,1)}) %all-gather.7.cloned.1.call-update) | async-done | bytes 33554448 | tf_op jit(solution)/shard_map/all_gather | solution.py:20
  649.3 13.4 %convolution_convert_fusion = bf16[96,4096]{1,0:T(8,128)(2,1)S(1)} fusion(bf16[1,96,4096]{2,1,0:T(8,128)(2,1)S(1)} %all-gather, bf16[1,4096,4096]{2,1,0:T(8,128)(2,1)} %all-gather.7.cloned.1.call-done), kind=kOutput, calls=%fused_computation.2 | convolution fusion | flops 3221618688 | bytes 35127296 | tf_op jit(solution)/shard_map/dot_general | solution.py:26
  662.7 1.6 collective-permute-start
  664.3 1.8 collective-permute-done
  666.2 0.0 copy-start
  666.2 0.9 copy-done
  667.1 0.0 all-gather.5.cloned.1.call-update
  667.1 0.0 reduce-scatter.2.cloned.1.call-start
  667.2 0.0 copy-done.2
  667.2 0.0 copy-done.3
  667.2 0.8 fusion.41
  673.7 0.1 fusion.38
  673.9 92.4 %all-gather.5.cloned.1.call-done = bf16[768,4096]{1,0:T(8,128)(2,1)} async-done(((bf16[96,4096]{1,0:T(8,128)(2,1)}), bf16[768,4096]{1,0:T(8,128)(2,1)}) %all-gather.5.cloned.1.call-update) | async-done | bytes 6291472 | tf_op jit(solution)/shard_map/all_gather | solution.py:46
  766.3 3.4 fusion.52
  769.8 1.2 fusion.8
  771.0 0.8 fusion.9
  771.7 1.1 fusion.30
  772.9 9.9 %fusion = f32[96,4096]{1,0:T(8,128)} fusion(bf16[96,2048]{1,0:T(8,128)(2,1)S(1)} %bitcast.91, bf16[4096,4096]{1,0:T(8,128)(2,1)} %bitcast.87), kind=kOutput, calls=%fused_computation | convolution fusion | flops 1610612736 | bytes 18743296 | tf_op jit(solution)/shard_map/dot_general | solution.py:68
  782.8 0.0 reduce-scatter.2.cloned.1.call-update
  782.8 24.5 %reduce-scatter.2.cloned.1.call-done = f32[96,2048]{1,0:T(8,128)} async-done(((f32[96,4096]{1,0:T(8,128)}), f32[96,2048]{1,0:T(8,128)}) %reduce-scatter.2.cloned.1.call-update) | async-done | bytes 786448 | tf_op jit(solution)/shard_map/reduce_scatter | solution.py:71
  807.3 1.9 select_bitcast_fusion
  (6 shorter events, 0.1 us)
Async XLA Ops:
  6.5 1.0 copy-start.1
  6.5 642.8 %all-gather.7.cloned.1.call-start = ((), (), s32[]{:S(2)}) async-start(), calls=%async_computation.3 | async-start | bytes 37748736 | tf_op jit(solution)/shard_map/all_gather | solution.py:20
  7.3 759.1 %all-gather.5.cloned.1.call-start = ((), (), s32[]{:S(2)}) async-start(), calls=%async_computation.1 | async-start | bytes 7077888 | tf_op jit(solution)/shard_map/all_gather | solution.py:46
  20.3 646.9 %copy-start.2 = (s32[8,3]{0,1:T(4,128)S(1)}, s32[8,3]{0,1:T(4,128)}, u32[]{:S(2)}) copy-start(s32[8,3]{0,1:T(4,128)} %param.6) | copy-start | bytes 292
  20.3 647.0 %copy-start.3 = (s32[8,3]{0,1:T(4,128)S(1)}, s32[8,3]{0,1:T(4,128)}, u32[]{:S(2)}) copy-start(s32[8,3]{0,1:T(4,128)} %param.7) | copy-start | bytes 292
  662.7 3.5 collective-permute-start
  666.2 0.9 copy-start
  667.1 140.2 %reduce-scatter.2.cloned.1.call-start = ((), (), s32[]{:S(2)}) async-start(), calls=%async_computation.2 | async-start | bytes 2359296 | tf_op jit(solution)/shard_map/reduce_scatter | solution.py:71
Sparse Core Ops, SparseCore 0:
  8.9 640.3 all-gather.6
  667.3 99.0 all-gather.4
  782.9 24.3 reduce-scatter.1
where the time goes:
time: 816 us
  waiting for transfers between devices  749 us (92%)
  matrix products  25.6 us (3%)
  between operations  18.8 us (2%)
  blocking collectives  12.7 us (2%)
    all_gather x1, waiting for transfers between devices, on_device(): weight = lax.all_gather(pool_weight[0], 'group', axis=0, tiled=True)  629 us
    all_gather x1, waiting for transfers between devices, on_device(): piece = lax.all_gather(moved, 'group', axis=0, tiled=True)  92.4 us
    reduce_scatter x1, waiting for transfers between devices, on_device(): lax.psum_scatter(partial_out, 'head', scatter_dimension=1, tiled=True)  24.5 us
  transfers between devices with their start and end apart: 4, of which 4 were waited for; matrix products, arithmetic and copies ran while one was open for 0% of the time, Pallas kernels for 0%

commit v1 on v0

--- a/solution.py
+++ b/solution.py
@@ -4,6 +4,17 @@
 from jax.sharding import PartitionSpec as P
 
 HEAD_DIM = 256
+
+
+def pass_along(x, mesh_axis, dim):
+    n_dev = lax.axis_size(mesh_axis)
+    forward = [(i, (i + 1) % n_dev) for i in range(n_dev)]
+    parts = [x]
+    for stride in range(1, n_dev):
+        parts = [lax.ppermute(parts[0], mesh_axis, forward), *parts]
+    whole = jnp.concatenate(parts, axis=dim)
+    shift = (lax.axis_index(mesh_axis) + 1) * parts[-1].shape[dim]
+    return jnp.roll(whole, shift, axis=dim)
 
 
 def shifted(value, axis, by):
@@ -17,7 +28,7 @@
     group_index = lax.axis_index("group")
     requests = lengths.shape[1]
     gathered = lax.all_gather(pool_rows[0], "head", axis=0, tiled=True)
-    weight = lax.all_gather(pool_weight[0], "group", axis=0, tiled=True)
+    weight = pass_along(pool_weight[0], "group", 0)
     mem_g = gathered.shape[0]
     wide = weight.shape[1] // 2
     heads_dev = wide // HEAD_DIM

time: 816 us -> 886 us (1.086)
  local copies, waits for them, and re-layouts: 4.64 us -> 67 us
    ppermute x0 -> x7, waiting for transfers between devices: none -> 639 us  [pass_along(): parts = [lax.ppermute(parts[0], mesh_axis, forward), *parts]]
    all_gather x1 -> x0, waiting for transfers between devices: 629 us -> none  [on_device(): weight = lax.all_gather(pool_weight[0], 'group', axis=0, tiled=True)]
    unnamed x8 -> x43, local copies, waits for them, and re-layouts: 1.16 us -> 61.3 us
  transfers between devices with their start and end apart: 4 -> 10, of which waited for: 4 -> 10; matrix products, arithmetic and copies ran while one was open for 0% -> 0% of each run, Pallas kernels for 0% -> 0%
where the time goes in v1:
time: 886 us; the launch traced here: 885 us
  waiting for transfers between devices  754 us (85%)
  local copies, waits for them, and re-layouts  67 us (8%)
  matrix products  28 us (3%)
  between operations  19.3 us (2%)
    ppermute x7, waiting for transfers between devices, pass_along(): parts = [lax.ppermute(parts[0], mesh_axis, forward), *parts]  639 us
    all_gather x1, waiting for transfers between devices, on_device(): piece = lax.all_gather(moved, 'group', axis=0, tiled=True)  88.1 us
    unnamed x43, local copies, waits for them, and re-layouts  61.3 us
    reduce_scatter x1, waiting for transfers between devices, on_device(): lax.psum_scatter(partial_out, 'head', scatter_dimension=1, tiled=True)  24.5 us
  transfers between devices with their start and end apart: 10, of which 10 were waited for; matrix products, arithmetic and copies ran while one was open for 0% of the time, Pallas kernels for 0%

profile of v1, /device:TPU:0, one launch (start us, length us, event | category | flops | bytes accessed | tf_op | source)
XLA Modules:
  0.0 885.0 jit_solution(11832674673785233724)
XLA Ops:
  6.5 0.0 all-gather.3.cloned.1.call-start
  6.5 3.0 collective-permute-start
  9.5 93.8 %collective-permute-done = bf16[512,4096]{1,0:T(8,128)(2,1)S(1)} collective-permute-done((bf16[512,4096]{1,0:T(8,128)(2,1)}, bf16[512,4096]{1,0:T(8,128)(2,1)S(1)}, u32[]{:S(2)}, u32[]{:S(2)}) %collective-permute-start) | collective-permute-done | bytes 4194336 | tf_op jit(solution)/shard_map/ppermute | solution.py:14
  103.3 0.0 copy-start.1
  103.4 2.0 copy-done.1
  105.3 0.0 collective-permute-start.1
  105.3 94.4 %collective-permute-done.1 = bf16[512,4096]{1,0:T(8,128)(2,1)S(1)} collective-permute-done((bf16[512,4096]{1,0:T(8,128)(2,1)S(1)}, bf16[512,4096]{1,0:T(8,128)(2,1)S(1)}, u32[]{:S(2)}, u32[]{:S(2)}) %collective-permute-start.1) | collective-permute-done | bytes 4194336 | tf_op jit(solution)/shard_map/ppermute | solution.py:14
  199.7 0.0 copy-start.3
  199.7 2.0 copy-done.3
  201.7 0.0 collective-permute-start.2
  201.7 93.6 %collective-permute-done.2 = bf16[512,4096]{1,0:T(8,128)(2,1)S(1)} collective-permute-done((bf16[512,4096]{1,0:T(8,128)(2,1)S(1)}, bf16[512,4096]{1,0:T(8,128)(2,1)S(1)}, u32[]{:S(2)}, u32[]{:S(2)}) %collective-permute-start.2) | collective-permute-done | bytes 4194336 | tf_op jit(solution)/shard_map/ppermute | solution.py:14
  295.3 2.0 copy-done.5
  297.3 0.0 collective-permute-start.3
  297.3 92.7 %collective-permute-done.3 = bf16[512,4096]{1,0:T(8,128)(2,1)S(1)} collective-permute-done((bf16[512,4096]{1,0:T(8,128)(2,1)S(1)}, bf16[512,4096]{1,0:T(8,128)(2,1)S(1)}, u32[]{:S(2)}, u32[]{:S(2)}) %collective-permute-start.3) | collective-permute-done | bytes 4194336 | tf_op jit(solution)/shard_map/ppermute | solution.py:14
  390.0 1.9 copy-done.7
  391.9 0.0 collective-permute-start.4
  391.9 91.9 %collective-permute-done.4 = bf16[512,4096]{1,0:T(8,128)(2,1)S(1)} collective-permute-done((bf16[512,4096]{1,0:T(8,128)(2,1)S(1)}, bf16[512,4096]{1,0:T(8,128)(2,1)S(1)}, u32[]{:S(2)}, u32[]{:S(2)}) %collective-permute-start.4) | collective-permute-done | bytes 4194336 | tf_op jit(solution)/shard_map/ppermute | solution.py:14
  483.8 1.9 copy-done.9
  485.7 0.0 collective-permute-start.5
  485.7 91.1 %collective-permute-done.5 = bf16[512,4096]{1,0:T(8,128)(2,1)} collective-permute-done((bf16[512,4096]{1,0:T(8,128)(2,1)S(1)}, bf16[512,4096]{1,0:T(8,128)(2,1)}, u32[]{:S(2)}, u32[]{:S(2)}) %collective-permute-start.5) | collective-permute-done | bytes 4194336 | tf_op jit(solution)/shard_map/ppermute | solution.py:14
  576.8 0.0 collective-permute-start.6
  576.8 8.6 all-gather
  585.5 81.8 %collective-permute-done.6 = bf16[512,4096]{1,0:T(8,128)(2,1)} collective-permute-done((bf16[512,4096]{1,0:T(8,128)(2,1)}, bf16[512,4096]{1,0:T(8,128)(2,1)}, u32[]{:S(2)}, u32[]{:S(2)}) %collective-permute-start.6) | collective-permute-done | bytes 4194336 | tf_op jit(solution)/shard_map/ppermute | solution.py:14
  667.3 4.6 constant_dynamic-update-slice_fusion.15
  671.9 4.8 constant_dynamic-update-slice_fusion.14
  676.7 0.0 copy-done.10
  676.7 2.4 constant_dynamic-update-slice_fusion.13
  679.1 1.3 copy-done.8
  680.4 2.4 constant_dynamic-update-slice_fusion.12
  682.8 1.3 copy-done.6
  684.1 2.4 constant_dynamic-update-slice_fusion.11
  686.5 1.3 copy-done.4
  687.8 2.4 constant_dynamic-update-slice_fusion.10
  690.2 1.3 copy-done.2
  691.5 2.4 constant_dynamic-update-slice_fusion.9
  694.0 1.3 copy-done
  695.2 2.2 constant_dynamic-update-slice_fusion.8
  697.5 4.7 constant_dynamic-update-slice_fusion.7
  702.2 4.6 constant_dynamic-update-slice_fusion.6
  706.8 2.2 constant_dynamic-update-slice_fusion.5
  709.0 2.2 constant_dynamic-update-slice_fusion.4
  711.2 2.3 constant_dynamic-update-slice_fusion.3
  713.5 2.2 constant_dynamic-update-slice_fusion.2
  715.8 2.2 constant_dynamic-update-slice_fusion.1
  717.9 2.2 constant_dynamic-update-slice_fusion
  720.2 13.5 %fusion.7 = bf16[96,4096]{1,0:T(8,128)(2,1)S(1)} fusion(bf16[8192,4096]{1,0:T(8,128)(2,1)} %constant_dynamic-update-slice_fusion, s32[]{:T(128)S(6)} %select_n.123, bf16[1,96,4096]{2,1,0:T(8,128)(2,1)S(1)} %all-gather), kind=kOutput, calls=%fused_computation.5 | convolution fusion | flops 3221618688 | bytes 35127300 | tf_op jit(solution)/shard_map/dot_general | solution.py:37
  733.7 1.3 collective-permute-start.7
  735.0 1.8 collective-permute-done.7
  736.9 0.9 copy-done.11
  737.8 0.0 all-gather.3.cloned.1.call-update
  737.8 0.2 reduce-scatter.2.cloned.1.call-start
  738.0 0.0 copy-done.12
  738.1 0.0 copy-done.13
  738.1 0.8 fusion.49
  744.7 0.1 fusion.46
  744.9 88.1 %all-gather.3.cloned.1.call-done = bf16[768,4096]{1,0:T(8,128)(2,1)} async-done(((bf16[96,4096]{1,0:T(8,128)(2,1)}), bf16[768,4096]{1,0:T(8,128)(2,1)}) %all-gather.3.cloned.1.call-update) | async-done | bytes 6291472 | tf_op jit(solution)/shard_map/all_gather | solution.py:57
  833.0 3.4 fusion.60
  836.4 1.2 fusion.16
  837.6 0.8 fusion.17
  838.4 1.1 fusion.38
  839.5 12.2 %fusion.2 = f32[96,4096]{1,0:T(8,128)} fusion(bf16[96,2048]{1,0:T(8,128)(2,1)S(1)} %bitcast.93, bf16[8192,4096]{1,0:T(8,128)(2,1)} %constant_dynamic-update-slice_fusion, s32[]{:T(128)S(6)} %select_n.123, s32[]{:T(128)S(6)} %add.50), kind=kOutput, calls=%fused_computation.2 | convolution fusion | flops 1610612736 | bytes 18743304 | tf_op jit(solution)/shard_map/dot_general | solution.py:79
  851.7 0.0 reduce-scatter.2.cloned.1.call-update
  851.7 24.5 %reduce-scatter.2.cloned.1.call-done = f32[96,2048]{1,0:T(8,128)} async-done(((f32[96,4096]{1,0:T(8,128)}), f32[96,2048]{1,0:T(8,128)}) %reduce-scatter.2.cloned.1.call-update) | async-done | bytes 786448 | tf_op jit(solution)/shard_map/reduce_scatter | solution.py:82
  876.2 1.9 select_bitcast_fusion
  (18 shorter events, 0.1 us)
Async XLA Ops:
  6.5 826.4 %all-gather.3.cloned.1.call-start = ((), (), s32[]{:S(2)}) async-start(), calls=%async_computation.1 | async-start | bytes 7077888 | tf_op jit(solution)/shard_map/all_gather | solution.py:57
  6.5 96.8 %collective-permute-start = (bf16[512,4096]{1,0:T(8,128)(2,1)}, bf16[512,4096]{1,0:T(8,128)(2,1)S(1)}, u32[]{:S(2)}, u32[]{:S(2)}) collective-permute-start(bf16[512,4096]{1,0:T(8,128)(2,1)} %bitcast.89), channel_id=1, source_target_pairs={{0,2},{2,4},{4,6},{6,8},{8,10},{10,12},{12,14},{14,0},{1,3},{3,5},... | collective-permute-start | bytes 12582920 | tf_op jit(solution)/shard_map/ppermute | solution.py:14
  103.3 2.0 copy-start.1
  105.3 94.4 %collective-permute-start.1 = (bf16[512,4096]{1,0:T(8,128)(2,1)S(1)}, bf16[512,4096]{1,0:T(8,128)(2,1)S(1)}, u32[]{:S(2)}, u32[]{:S(2)}) collective-permute-start(bf16[512,4096]{1,0:T(8,128)(2,1)S(1)} %collective-permute-done), channel_id=1, source_target_pairs={{0,2},{2,4},{4,6},{6,8},{8,10},{10,12},{12,14},{14,0},{1,3},{3,5},... | collective-permute-start | bytes 12582920 | tf_op jit(solution)/shard_map/ppermute | solution.py:14
  199.7 2.0 copy-start.3
  201.7 93.6 %collective-permute-start.2 = (bf16[512,4096]{1,0:T(8,128)(2,1)S(1)}, bf16[512,4096]{1,0:T(8,128)(2,1)S(1)}, u32[]{:S(2)}, u32[]{:S(2)}) collective-permute-start(bf16[512,4096]{1,0:T(8,128)(2,1)S(1)} %collective-permute-done.1), channel_id=1, source_target_pairs={{0,2},{2,4},{4,6},{6,8},{8,10},{10,12},{12,14},{14,0},{1,3},{3,5},... | collective-permute-start | bytes 12582920 | tf_op jit(solution)/shard_map/ppermute | solution.py:14
  295.3 2.0 copy-start.5
  297.3 92.7 %collective-permute-start.3 = (bf16[512,4096]{1,0:T(8,128)(2,1)S(1)}, bf16[512,4096]{1,0:T(8,128)(2,1)S(1)}, u32[]{:S(2)}, u32[]{:S(2)}) collective-permute-start(bf16[512,4096]{1,0:T(8,128)(2,1)S(1)} %collective-permute-done.2), channel_id=1, source_target_pairs={{0,2},{2,4},{4,6},{6,8},{8,10},{10,12},{12,14},{14,0},{1,3},{3,5},... | collective-permute-start | bytes 12582920 | tf_op jit(solution)/shard_map/ppermute | solution.py:14
  390.0 1.9 copy-start.7
  391.9 91.9 %collective-permute-start.4 = (bf16[512,4096]{1,0:T(8,128)(2,1)S(1)}, bf16[512,4096]{1,0:T(8,128)(2,1)S(1)}, u32[]{:S(2)}, u32[]{:S(2)}) collective-permute-start(bf16[512,4096]{1,0:T(8,128)(2,1)S(1)} %collective-permute-done.3), channel_id=1, source_target_pairs={{0,2},{2,4},{4,6},{6,8},{8,10},{10,12},{12,14},{14,0},{1,3},{3,5},... | collective-permute-start | bytes 12582920 | tf_op jit(solution)/shard_map/ppermute | solution.py:14
  483.8 1.9 copy-start.9
  485.7 91.1 %collective-permute-start.5 = (bf16[512,4096]{1,0:T(8,128)(2,1)S(1)}, bf16[512,4096]{1,0:T(8,128)(2,1)}, u32[]{:S(2)}, u32[]{:S(2)}) collective-permute-start(bf16[512,4096]{1,0:T(8,128)(2,1)S(1)} %collective-permute-done.4), channel_id=1, source_target_pairs={{0,2},{2,4},{4,6},{6,8},{8,10},{10,12},{12,14},{14,0},{1,3},{3,5},... | collective-permute-start | bytes 12582920 | tf_op jit(solution)/shard_map/ppermute | solution.py:14
  576.8 90.5 %collective-permute-start.6 = (bf16[512,4096]{1,0:T(8,128)(2,1)}, bf16[512,4096]{1,0:T(8,128)(2,1)}, u32[]{:S(2)}, u32[]{:S(2)}) collective-permute-start(bf16[512,4096]{1,0:T(8,128)(2,1)} %collective-permute-done.5), channel_id=1, source_target_pairs={{0,2},{2,4},{4,6},{6,8},{8,10},{10,12},{12,14},{14,0},{1,3},{3,5},... | collective-permute-start | bytes 12582920 | tf_op jit(solution)/shard_map/ppermute | solution.py:14
  671.9 4.8 copy-start.10
  676.7 3.7 copy-start.8
  680.4 3.7 copy-start.6
  684.1 3.7 copy-start.4
  687.8 3.7 copy-start.2
  691.5 3.7 copy-start
  720.1 17.9 %copy-start.12 = (s32[8,3]{0,1:T(4,128)S(1)}, s32[8,3]{0,1:T(4,128)}, u32[]{:S(2)}) copy-start(s32[8,3]{0,1:T(4,128)} %param.6) | copy-start | bytes 292
  720.2 18.0 %copy-start.13 = (s32[8,3]{0,1:T(4,128)S(1)}, s32[8,3]{0,1:T(4,128)}, u32[]{:S(2)}) copy-start(s32[8,3]{0,1:T(4,128)} %param.7) | copy-start | bytes 292
  733.7 3.2 collective-permute-start.7
  736.9 0.9 copy-start.11
  737.8 138.4 %reduce-scatter.2.cloned.1.call-start = ((), (), s32[]{:S(2)}) async-start(), calls=%async_computation.2 | async-start | bytes 2359296 | tf_op jit(solution)/shard_map/reduce_scatter | solution.py:82
Sparse Core Ops, SparseCore 0:
  737.9 94.9 all-gather.2
  851.9 24.3 reduce-scatter.1
